TPU v7x, 512 devices: a whole 4x8x8 slice. The times are simulated.
512 devices in a mesh: row: 16 (over x, z_hi), col: 8 (over y), mat: 4 (over z_lo, core).
Axes of the slice: x: 4, y: 8, z: 8 (z_hi: 4, z_lo: 2; z = z_hi * 2 + z_lo), core: 2. Of those that a mesh axis runs over, the one named last changes fastest.
Arguments:
- grads: float32 [4, 4096, 4096], P('mat', 'row', 'col'), may hold values from -6 to 6
- left_stats: float32 [4, 4096, 256], P('mat', 'row'), as said below
- right_stats: float32 [4, 4096, 256], P('mat', 'col'), as said below
Outputs:
- update: float32 [4, 4096, 4096], P('mat', ('row', 'col'))
Inputs may be any that keep to these rules, and one draw needn't show every extreme that they name: `left_stats`: each aligned block of 256 rows along the second dimension, taken as a 256 x 256 matrix, is symmetric positive definite. `right_stats`: each aligned block of 256 rows along the second dimension, taken as a 256 x 256 matrix, is symmetric positive definite.
All inputs are finite; a program needn't handle non-finite values.
Results may differ from a plain program's by a relative error of at most 0.00011.
Values sent between devices are 32-bit elements; how exact they have to be, the bound alone decides.
A program may use at most 64 MiB of HBM per device.

v0:
```python
import jax
import jax.numpy as jnp
from jax import lax
from jax.sharding import PartitionSpec as P

D = 4096
ITERS = 3


beta_mix = 0.5
eps_shift = 0.001


def sent_to_all(value, axis):
    size = lax.axis_size(axis)
    return lax.all_to_all(
        jnp.broadcast_to(value[None], (size, *value.shape)), axis, 0, 0, tiled=True
    )


def taken_together(value, axis):
    return sent_to_all(value, axis).sum(axis=0)


def in_blocks(value, dim, size):
    before, after = (value.shape[:dim], value.shape[dim + 1 :])
    return jnp.moveaxis(value.reshape(*before, size, -1, *after), dim, 0)


def sent_and_summed(value, axis, dim):
    blocks = in_blocks(value, dim, lax.axis_size(axis))
    arrived = lax.all_to_all(blocks, axis, split_axis=0, concat_axis=0, tiled=True)
    return arrived.sum(axis=0)


def filled_up(lines, size):
    spare = -lines.shape[0] % size
    if not spare:
        return lines
    return jnp.concatenate([lines, jnp.zeros((spare, *lines.shape[1:]), lines.dtype)])


def laid_out(blocks, dim):
    blocks = jnp.moveaxis(blocks, 0, dim)
    dims = blocks.shape
    return blocks.reshape(*dims[:dim], dims[dim] * dims[dim + 1], *dims[dim + 2 :])


def gathered_copies(value, axis, dim):
    blocks = sent_to_all(value, axis)
    return laid_out(blocks, dim)


def sum_by_parts(value, axes):
    lines = value.reshape(-1, value.shape[-1])
    own = sent_and_summed(filled_up(lines, lax.axis_size(axes)), axes, 0)
    whole = gathered_copies(own, axes, 0)
    return whole[: len(lines)].reshape(value.shape)


def matmul(left, right):
    return jnp.einsum("...ij,...jk->...ik", left, right, precision=lax.Precision.HIGHEST)


def newton_root(factor):
    size = factor.shape[-1]
    ident = jnp.eye(size, dtype=jnp.float32)
    scale = jnp.sqrt(jnp.sum(factor * factor, axis=(-2, -1), keepdims=True))
    moving = factor / scale
    result = jnp.broadcast_to(ident, factor.shape)
    for count in range(ITERS):
        step_mat = (5.0 * ident - moving) * 0.25
        result = matmul(result, step_mat)
        squared = matmul(step_mat, step_mat)
        moving = matmul(matmul(squared, squared), moving)
    return result * jnp.power(scale, -0.25)


def per_device(grads, left_stats, right_stats):
    mats, tile_rows, tile_cols = grads.shape
    blk = left_stats.shape[2]
    row_blocks = tile_rows // blk
    col_blocks = tile_cols // blk
    ident = jnp.eye(blk, dtype=jnp.float32)
    by_rows = grads.reshape(mats, row_blocks, blk, tile_cols)
    left_part = jnp.einsum("mibd,mied->mibe", by_rows, by_rows, precision=lax.Precision.HIGHEST) / D
    by_cols = grads.reshape(mats, tile_rows, col_blocks, blk)
    right_part = (
        jnp.einsum("mdjb,mdje->mjbe", by_cols, by_cols, precision=lax.Precision.HIGHEST) / D
    )
    left_gram = taken_together(left_part, "col")
    right_gram = sum_by_parts(right_part, "row")
    left_factor = (
        beta_mix * left_stats.reshape(mats, row_blocks, blk, blk)
        + (1.0 - beta_mix) * left_gram
        + eps_shift * ident
    )
    right_factor = (
        beta_mix * right_stats.reshape(mats, col_blocks, blk, blk)
        + (1.0 - beta_mix) * right_gram
        + eps_shift * ident
    )
    left_root = newton_root(left_factor)
    right_root = newton_root(right_factor)
    half = jnp.einsum("mibe,mied->mibd", left_root, by_rows, precision=lax.Precision.HIGHEST)
    half = half.reshape(mats, tile_rows, col_blocks, blk)
    full = jnp.einsum("mdjb,mjbe->mdje", half, right_root, precision=lax.Precision.HIGHEST)
    full = full.reshape(mats, tile_rows, tile_cols)
    return lax.all_to_all(full, "col", split_axis=1, concat_axis=2, tiled=True)


def solution(mesh):
    return jax.shard_map(
        per_device,
        mesh=mesh,
        in_specs=(P("mat", "row", "col"), P("mat", "row", None), P("mat", "col", None)),
        out_specs=P("mat", ("row", "col"), None),
        check_vma=False,
    )
```

profile of v0, /device:TPU:65, one launch (start us, length us, event | category | flops | bytes accessed | tf_op | source)
XLA Modules:
  0.0 144.1 jit_solution(17749709026194187821)
XLA Ops:
  0.0 1.4 reshape.282
  1.4 1.1 convolution_multiply_fusion.1
  2.4 28.7 %all_to_all.33 = f32[16,32,256]{2,1,0:T(8,128)S(1)} all-to-all(f32[16,32,256]{2,1,0:T(8,128)S(1)} %bitcast.106), channel_id=1, replica_groups=mesh['row'=16,'col'=8,'mat'=4] {'row'}, dimensions={0} | all-to-all | bytes 1048576 | tf_op jit(solution)/shard_map/all_to_all | solution.py:32
  31.1 0.8 broadcast_in_dim.7
  32.0 5.3 %all-to-all-start.1 = ((f32[16,32,256]{2,1,0:T(8,128)}), f32[16,32,256]{2,1,0:T(8,128)S(1)}, u32[]{:S(2)}, u32[]{:S(2)}) async-start(f32[16,32,256]{2,1,0:T(8,128)} %broadcast_in_dim.7), calls=%async_computation.1 | async-start | bytes 1048576 | tf_op jit(solution)/shard_map/all_to_all | solution.py:16
  38.0 17.6 %all-to-all-done.1 = f32[16,32,256]{2,1,0:T(8,128)S(1)} async-done(((f32[16,32,256]{2,1,0:T(8,128)}), f32[16,32,256]{2,1,0:T(8,128)S(1)}, u32[]{:S(2)}, u32[]{:S(2)}) %all-to-all-start.1) | async-done | bytes 524320 | tf_op jit(solution)/shard_map/all_to_all | solution.py:16
  55.6 1.5 %broadcast_in_dim.8 = f32[8,1,1,256,256]{4,3,2,1,0:T(8,128)} broadcast(f32[256,256]{1,0:T(8,128)S(1)} %convolution_multiply_fusion.3), dimensions={3,4} | broadcast | bytes 2359296 | tf_op jit(solution)/shard_map/broadcast_in_dim | solution.py:17
  57.1 6.8 %all-to-all-start.2 = ((f32[8,1,1,256,256]{4,3,2,1,0:T(8,128)}), f32[8,1,1,256,256]{4,3,2,1,0:T(8,128)S(1)}, u32[]{:S(2)}, u32[]{:S(2)}) async-start(f32[8,1,1,256,256]{4,3,2,1,0:T(8,128)} %broadcast_in_dim.8), calls=%async_computation.2 | async-start | bytes 4194304 | tf_op jit(solution)/shard_map/all_to_all | solution.py:16
  63.9 1.0 copy.29
  65.0 1.2 fusion.5
  66.4 1.2 fusion.9
  67.6 0.7 fusion.11
  68.3 0.7 fusion.80
  69.0 0.7 fusion.81
  69.6 0.7 fusion.13
  70.4 0.6 fusion.82
  71.7 0.7 fusion
  72.3 0.7 fusion.14
  73.1 0.7 convolution_multiply_fusion
  73.7 41.9 %all-to-all-done.2 = f32[8,1,1,256,256]{4,3,2,1,0:T(8,128)S(1)} async-done(((f32[8,1,1,256,256]{4,3,2,1,0:T(8,128)}), f32[8,1,1,256,256]{4,3,2,1,0:T(8,128)S(1)}, u32[]{:S(2)}, u32[]{:S(2)}) %all-to-all-start.2) | async-done | bytes 2097184 | tf_op jit(solution)/shard_map/all_to_all | solution.py:16
  115.8 0.8 multiply_reduce_fusion
  121.6 1.0 fusion.86
  123.0 20.2 %all_to_all.34 = f32[1,256,512]{2,0,1:T(1,128)S(1)} all-to-all(f32[1,256,512]{2,0,1:T(1,128)S(1)} %copy.26), channel_id=1, replica_groups=mesh['row'=16,'col'=8,'mat'=4] {'col'}, dimensions={1} | all-to-all | bytes 1048576 | tf_op jit(solution)/shard_map/all_to_all | solution.py:109
  143.3 0.8 copy.31
  (29 shorter events, 6.3 us)
Async XLA Ops:
  1.4 36.0 %copy-start = (f32[1,256,512]{2,1,0:T(8,128)S(1)}, f32[1,256,512]{2,1,0:T(8,128)}, u32[]{:S(2)}) copy-start(f32[1,256,512]{2,1,0:T(8,128)} %param.3) | copy-start | bytes 1572868
  32.0 23.6 %all-to-all-start.1 = ((f32[16,32,256]{2,1,0:T(8,128)}), f32[16,32,256]{2,1,0:T(8,128)S(1)}, u32[]{:S(2)}, u32[]{:S(2)}) async-start(f32[16,32,256]{2,1,0:T(8,128)} %broadcast_in_dim.7), calls=%async_computation.1 | async-start | bytes 1048576 | tf_op jit(solution)/shard_map/all_to_all | solution.py:16
  57.1 58.5 %all-to-all-start.2 = ((f32[8,1,1,256,256]{4,3,2,1,0:T(8,128)}), f32[8,1,1,256,256]{4,3,2,1,0:T(8,128)S(1)}, u32[]{:S(2)}, u32[]{:S(2)}) async-start(f32[8,1,1,256,256]{4,3,2,1,0:T(8,128)} %broadcast_in_dim.8), calls=%async_computation.2 | async-start | bytes 4194304 | tf_op jit(solution)/shard_map/all_to_all | solution.py:16
  73.0 42.7 %copy-start.2 = (f32[1,256,256]{2,1,0:T(8,128)S(1)}, f32[1,256,256]{2,1,0:T(8,128)}, u32[]{:S(2)}) copy-start(f32[1,256,256]{2,1,0:T(8,128)} %param.4) | copy-start | bytes 786436
  118.9 2.1 %copy-start.1 = (f32[512,256]{1,0:T(8,128)S(1)}, f32[512,256]{1,0:T(8,128)}, u32[]{:S(2)}) copy-start(f32[512,256]{1,0:T(8,128)} %copy.29) | copy-start | bytes 1572868
where the time goes:
time: 145 us; the launch traced here: 144 us
  waiting for transfers between devices  59.5 us (41%)
  blocking collectives  48.9 us (34%)
  matrix products  13 us (9%)
  starting transfers between devices  12.2 us (8%)
  local copies, waits for them, and re-layouts  6.08 us (4%)
  other arithmetic  3.48 us (2%)
    all_to_all x2, waiting for transfers between devices, sent_to_all(): lax.all_to_all(jnp.broadcast_to(value[None], (size, *value.shape)), axis,...  59.5 us
    all_to_all x1, blocking collectives, sent_and_summed(): lax.all_to_all(blocks, axis, split_axis=0, concat_axis=0, tiled=True)  28.7 us
    all_to_all x1, blocking collectives, per_device(): return lax.all_to_all(full, 'col', split_axis=1, concat_axis=2, tiled=True)  20.2 us
    all_to_all x2, starting transfers between devices, sent_to_all(): lax.all_to_all(jnp.broadcast_to(value[None], (size, *value.shape)), axis,...  12.2 us
    dot_general x18, matrix products, matmul(): jnp.einsum('...ij,...jk->...ik', left, right, precision=lax.Precision.HIG...  9.62 us
  transfers between devices with their start and end apart: 2, of which 2 were waited for; matrix products, arithmetic and copies ran while one was open for 7% of the time, Pallas kernels for 0%

commit v1 on v0

v1 whole, which is shorter than its diff:
```python
import jax
import jax.numpy as jnp
from jax import lax
from jax.experimental import pallas as pl
from jax.experimental.pallas import tpu as pltpu
from jax.sharding import PartitionSpec as P

D = 4096
BLK = 256
H = 128
NX, NZ, NY = 4, 4, 8
BETA, EPS = 0.5, 0.001
F32, BF16 = jnp.float32, jnp.bfloat16
MESH = pl.DeviceIdType.MESH
PACK = 3 * H
RP = PACK // (NX * NZ)
LP = PACK // NY
YORD = (4, 3, 5, 2, 6, 1, 7)
XORD = (2, 1, 3)
ZORD = (2, 1, 3)


def split(v):
    hi = v.astype(BF16)
    return hi, (v - hi.astype(F32)).astype(BF16)


def dot(a, b):
    return jnp.dot(a, b, preferred_element_type=F32)


def mm(a, b):
    return dot(a[0], b[0]) + (dot(a[0], b[1]) + dot(a[1], b[0]))


def pack(ref, v):
    ref[0:H, :] = v[:H, :H]
    ref[H : 2 * H, :] = v[:H, H:]
    ref[2 * H : 3 * H, :] = v[H:, H:]


def unpack(ref):
    a, b, d = ref[0:H, :], ref[H : 2 * H, :], ref[2 * H : 3 * H, :]
    top = jnp.concatenate([a, b], axis=1)
    low = jnp.concatenate([b.T, d], axis=1)
    return jnp.concatenate([top, low], axis=0)


def eye():
    rows = lax.broadcasted_iota(jnp.int32, (BLK, BLK), 0)
    cols = lax.broadcasted_iota(jnp.int32, (BLK, BLK), 1)
    return jnp.where(rows == cols, 1.0, 0.0).astype(F32)


def newton(gram, stats):
    ident = eye()
    factor = BETA * stats + ((1.0 - BETA) / D) * gram + EPS * ident
    ss = jnp.sum(jnp.sum(factor * factor, axis=0, keepdims=True), axis=1, keepdims=True)
    m0 = factor * (1.0 / jnp.sqrt(ss))
    t1 = split(1.25 * ident - 0.25 * m0)
    s1 = split(mm(t1, t1))
    q1 = split(mm(s1, s1))
    m1 = mm(q1, split(m0))
    t2 = split(1.25 * ident - 0.25 * m1)
    s2 = split(mm(t2, t2))
    x2 = mm(t1, t2)
    q2 = split(mm(s2, s2))
    y2 = split(mm(split(m1), split(x2)))
    x3 = 1.25 * x2 - 0.25 * mm(q2, y2)
    return x3, 1.0 / jnp.sqrt(jnp.sqrt(jnp.sqrt(ss)))


def kernel(
    g_hbm, ls_hbm, rs_hbm, o_ref,
    g, ls, rs, lp, rp, lrecv, xr, zs, zr, lag, rag, upd,
    in_sem, out_sem, ly_s, ly_r, lg_s, lg_r, x_s, x_r, z_s, z_r, gz_s, gz_r, gx_s, gx_r, u_s, u_r,
):
    row, col = lax.axis_index("row"), lax.axis_index("col")
    x, zh = row // NZ, lax.rem(row, NZ)

    def at_x(d):
        return lax.rem(x + d, NX)

    def at_z(e):
        return lax.rem(zh + e, NZ)

    def at_y(d):
        return lax.rem(col + d, NY)

    def to_x(d):
        return {"row": at_x(d) * NZ + zh, "col": col}

    def to_z(e):
        return {"row": x * NZ + at_z(e), "col": col}

    def to_y(d):
        return {"row": row, "col": at_y(d)}

    def send(src, dst, ss, rs_, device):
        copy = pltpu.make_async_remote_copy(
            src_ref=src, dst_ref=dst, send_sem=ss, recv_sem=rs_, device_id=device, device_id_type=MESH
        )
        copy.start()
        return copy

    loads = [
        pltpu.make_async_copy(g_hbm.at[0], g, in_sem.at[0]),
        pltpu.make_async_copy(rs_hbm.at[0], rs, in_sem.at[1]),
        pltpu.make_async_copy(ls_hbm.at[0], ls, in_sem.at[2]),
    ]
    for copy in loads:
        copy.start()
    barrier = pltpu.get_barrier_semaphore()
    greeted = [to_y(d) for d in YORD] + [to_z(e) for e in ZORD] + [to_x(d) for d in XORD]
    for device in greeted:
        pl.semaphore_signal(barrier, inc=1, device_id=device, device_id_type=MESH)

    loads[0].wait()
    tile = g[...]
    gh, gl = split(tile)
    th, tl = split(tile.T)
    for q in range(2):
        cols = slice(q * BLK, (q + 1) * BLK)
        pack(rp.at[q], mm((th[cols], tl[cols]), (gh[:, cols], gl[:, cols])))
    pack(lp, mm((gh, gl), (th, tl)))
    pl.semaphore_wait(barrier, len(greeted))

    sx, sl = {}, {}

    def right_over_x(q):
        for e in ZORD + (0,):
            for d in XORD:
                at = pl.multiple_of((at_x(d) * NZ + at_z(e)) * RP, 8)
                sx[q, d, e] = send(
                    rp.at[q, pl.ds(at, RP), :], xr.at[q, d - 1, e],
                    x_s.at[q, d - 1, e], x_r.at[q, d - 1, e], to_x(d),
                )

    right_over_x(0)
    for d in YORD:
        at = pl.multiple_of(at_y(d) * LP, 8)
        sl[d] = send(lp.at[pl.ds(at, LP), :], lrecv.at[d - 1], ly_s.at[d - 1], ly_r.at[d - 1], to_y(d))
    right_over_x(1)

    sz, kept = {}, {}
    for q in range(2):
        for e in ZORD + (0,):
            at = pl.multiple_of((x * NZ + at_z(e)) * RP, 8)
            total = rp[q, pl.ds(at, RP), :]
            for d in XORD:
                sx[q, d, e].wait_recv()
            for d in XORD:
                total = total + xr[q, d - 1, e]
            if e:
                zs[q, e - 1] = total
                sz[q, e] = send(zs.at[q, e - 1], zr.at[q, e - 1], z_s.at[q, e - 1], z_r.at[q, e - 1], to_z(e))
            else:
                kept[q] = total

    at = pl.multiple_of(col * LP, 8)
    total = lp[pl.ds(at, LP), :]
    for d in YORD:
        sl[d].wait_recv()
        total = total + lrecv[d - 1]
    lag[pl.ds(at, LP), :] = total
    sg = {}
    for d in YORD:
        sg[d] = send(lag.at[pl.ds(at, LP), :], lag.at[pl.ds(at, LP), :], lg_s.at[d - 1], lg_r.at[d - 1], to_y(d))

    gz, gx = {}, {}

    def spread_x(q, e):
        here = pl.multiple_of((x * NZ + lax.rem(zh - e + NZ, NZ)) * RP, 8)
        for d in XORD:
            gx[q, d, e] = send(
                rag.at[q, pl.ds(here, RP), :], rag.at[q, pl.ds(here, RP), :],
                gx_s.at[q, d - 1, e], gx_r.at[q, d - 1, e], to_x(d),
            )

    own = pl.multiple_of(row * RP, 8)
    for q in range(2):
        total = kept[q]
        for e in ZORD:
            sz[q, e].wait_recv()
            total = total + zr[q, e - 1]
        rag[q, pl.ds(own, RP), :] = total
        for e in ZORD:
            gz[q, e] = send(
                rag.at[q, pl.ds(own, RP), :], rag.at[q, pl.ds(own, RP), :],
                gz_s.at[q, e - 1], gz_r.at[q, e - 1], to_z(e),
            )
        spread_x(q, 0)
    for q in range(2):
        for e in (1, 3, 2):
            gz[q, e].wait_recv()
            spread_x(q, e)

    for d in YORD:
        sg[d].wait_recv()
    loads[2].wait()
    root, scale = newton(unpack(lag), ls[...])
    half = mm(split(root * scale), (gh, gl))

    loads[1].wait()
    su = {}
    for q in range(2):
        for e in range(NZ):
            for d in XORD:
                gx[q, d, e].wait_recv()
        root, scale = newton(unpack(rag.at[q]), rs[q * BLK : (q + 1) * BLK, :])
        upd[q] = mm(split(half[:, q * BLK : (q + 1) * BLK]), split(root * scale))
        lanes = pl.ds(pl.multiple_of(col * 2 * BLK + q * BLK, BLK), BLK)
        for d in YORD:
            at = pl.multiple_of(at_y(d) * 32, 32)
            su[q, d] = send(
                upd.at[q, pl.ds(at, 32), :], o_ref.at[0, :, lanes], u_s.at[q, d - 1], u_r.at[q, d - 1], to_y(d)
            )
        mine = pltpu.make_async_copy(
            upd.at[q, pl.ds(pl.multiple_of(col * 32, 32), 32), :], o_ref.at[0, :, lanes], out_sem.at[q]
        )
        mine.start()
        su[q, 0] = mine

    for q in range(2):
        su[q, 0].wait()
        for d in YORD:
            su[q, d].wait_recv()
    for group in (sx, sl, sz, sg, gz, gx):
        for copy in group.values():
            copy.wait_send()
    for (q, d), copy in su.items():
        if d:
            copy.wait_send()


def per_device(grads, left_stats, right_stats):
    dma = pltpu.SemaphoreType.DMA
    return pl.pallas_call(
        kernel,
        out_shape=jax.ShapeDtypeStruct((1, 32, D), F32),
        in_specs=[pl.BlockSpec(memory_space=pl.ANY)] * 3,
        out_specs=pl.BlockSpec(memory_space=pl.ANY),
        scratch_shapes=[
            pltpu.VMEM((BLK, 2 * BLK), F32),
            pltpu.VMEM((BLK, BLK), F32),
            pltpu.VMEM((2 * BLK, BLK), F32),
            pltpu.VMEM((PACK, H), F32),
            pltpu.VMEM((2, PACK, H), F32),
            pltpu.VMEM((NY - 1, LP, H), F32),
            pltpu.VMEM((2, NX - 1, NZ, RP, H), F32),
            pltpu.VMEM((2, NZ - 1, RP, H), F32),
            pltpu.VMEM((2, NZ - 1, RP, H), F32),
            pltpu.VMEM((PACK, H), F32),
            pltpu.VMEM((2, PACK, H), F32),
            pltpu.VMEM((2, BLK, BLK), F32),
            dma((3,)), dma((2,)),
            dma((NY - 1,)), dma((NY - 1,)), dma((NY - 1,)), dma((NY - 1,)),
            dma((2, NX - 1, NZ)), dma((2, NX - 1, NZ)),
            dma((2, NZ - 1)), dma((2, NZ - 1)), dma((2, NZ - 1)), dma((2, NZ - 1)),
            dma((2, NX - 1, NZ)), dma((2, NX - 1, NZ)),
            dma((2, NY - 1)), dma((2, NY - 1)),
        ],
        compiler_params=pltpu.CompilerParams(collective_id=0, has_side_effects=True),
        name="shampoo",
    )(grads, left_stats, right_stats)


def solution(mesh):
    return jax.shard_map(
        per_device,
        mesh=mesh,
        in_specs=(P("mat", "row", "col"), P("mat", "row", None), P("mat", "col", None)),
        out_specs=P("mat", ("row", "col"), None),
        check_vma=False,
    )
```

time: 145 us -> 47.8 us (0.33)
  the two profiles are of different devices: /device:TPU:65 before, /device:TPU:64 now
where the time goes in v1:
time: 47.8 us; the launch traced here: 47.6 us
  Pallas kernels  45.7 us (96%)
  local copies, waits for them, and re-layouts  1.87 us (4%)
    pallas_call x1, Pallas kernels, per_device(): pl.pallas_call(kernel, out_shape=jax.ShapeDtypeStruct((1, 32, D), F32), i...  45.7 us
    unnamed x1, local copies, waits for them, and re-layouts  1.87 us

profile of v1, /device:TPU:64, one launch (start us, length us, event | category | flops | bytes accessed | tf_op | source)
XLA Modules:
  0.0 47.6 jit_solution(9939816974276961644)
XLA Ops:
  0.0 45.7 %shampoo.1 = f32[1,32,4096]{2,1,0:T(8,128)} custom-call(f32[1,256,512]{2,1,0:T(8,128)} %g_hbm.1, f32[1,256,256]{2,1,0:T(8,128)} %ls_hbm.1, f32[1,512,256]{2,1,0:T(8,128)} %rs_hbm.1), custom_call_target="tpu_custom_call" | custom-call | tf_op jit(solution)/shard_map/shampoo/pallas_call | solution.py:238
  45.7 1.9 %copy.5 = f32[1,32,4096]{2,1,0:T(8,128)} copy(f32[1,32,4096]{2,1,0:T(8,128)} %shampoo.1) | data formatting | bytes 1048576

commit v2 on v1

v2 whole, which is shorter than its diff:
```python
import jax
import jax.numpy as jnp
from jax import lax
from jax.experimental import pallas as pl
from jax.experimental.pallas import tpu as pltpu
from jax.sharding import PartitionSpec as P

D = 4096
BLK = 256
H = 128
NX, NZ, NY = 4, 4, 8
BETA, EPS = 0.5, 0.001
F32, BF16 = jnp.float32, jnp.bfloat16
MESH = pl.DeviceIdType.MESH
PACK = 3 * H
XP = PACK // NX
NCH = 2
CR = XP // NCH
LP = PACK // NY
YORD = (4, 3, 5, 2, 6, 1, 7)
XORD = (2, 1, 3)
ZORD = (2, 1, 3)


def split(v):
    hi = v.astype(BF16)
    return hi, (v - hi.astype(F32)).astype(BF16)


def dot(a, b):
    return jnp.dot(a, b, preferred_element_type=F32)


def mm(a, b):
    return dot(a[0], b[0]) + (dot(a[0], b[1]) + dot(a[1], b[0]))


def pack(ref, v):
    ref[0:H, :] = v[:H, :H]
    ref[H : 2 * H, :] = v[:H, H:]
    ref[2 * H : 3 * H, :] = v[H:, H:]


def unpack(ref):
    a, b, d = ref[0:H, :], ref[H : 2 * H, :], ref[2 * H : 3 * H, :]
    top = jnp.concatenate([a, b], axis=1)
    low = jnp.concatenate([b.T, d], axis=1)
    return jnp.concatenate([top, low], axis=0)


def eye():
    rows = lax.broadcasted_iota(jnp.int32, (BLK, BLK), 0)
    cols = lax.broadcasted_iota(jnp.int32, (BLK, BLK), 1)
    return jnp.where(rows == cols, 1.0, 0.0).astype(F32)


def newton(*pairs):
    ident = eye()
    factors = [BETA * stats + ((1.0 - BETA) / D) * gram + EPS * ident for gram, stats in pairs]
    ss = [jnp.sum(jnp.sum(f * f, axis=0, keepdims=True), axis=1, keepdims=True) for f in factors]
    m0 = [f * (1.0 / jnp.sqrt(s)) for f, s in zip(factors, ss)]
    t1 = [split(1.25 * ident - 0.25 * m) for m in m0]
    s1 = [split(mm(t, t)) for t in t1]
    q1 = [split(mm(s, s)) for s in s1]
    m1 = [mm(q, split(m)) for q, m in zip(q1, m0)]
    t2 = [split(1.25 * ident - 0.25 * m) for m in m1]
    s2 = [split(mm(t, t)) for t in t2]
    x2 = [mm(a, b) for a, b in zip(t1, t2)]
    q2 = [split(mm(s, s)) for s in s2]
    y2 = [split(mm(split(m), split(v))) for m, v in zip(m1, x2)]
    x3 = [1.25 * v - 0.25 * mm(q, y) for v, q, y in zip(x2, q2, y2)]
    return [v * (1.0 / jnp.sqrt(jnp.sqrt(jnp.sqrt(s)))) for v, s in zip(x3, ss)]


def kernel(
    g_hbm, ls_hbm, rs_hbm, o_ref,
    g, ls, rs, gs, lp, rp, lrecv, xr, zs, zr, lag, rag, upd,
    in_sem, out_sem, ly_s, ly_r, lg_s, lg_r, x_s, x_r, z_s, z_r, gx_s, gx_r, u_s, u_r,
):
    row, col = lax.axis_index("row"), lax.axis_index("col")
    x, zh = row // NZ, lax.rem(row, NZ)

    def at_x(d):
        return lax.rem(x + d, NX)

    def at_z(e):
        return lax.rem(zh + e, NZ)

    def at_y(d):
        return lax.rem(col + d, NY)

    def to_x(d):
        return {"row": at_x(d) * NZ + zh, "col": col}

    def to_z(e):
        return {"row": x * NZ + at_z(e), "col": col}

    def to_y(d):
        return {"row": row, "col": at_y(d)}

    def send(src, dst, ss, rs_, device):
        copy = pltpu.make_async_remote_copy(
            src_ref=src, dst_ref=dst, send_sem=ss, recv_sem=rs_, device_id=device, device_id_type=MESH
        )
        copy.start()
        return copy

    loads = [
        pltpu.make_async_copy(g_hbm.at[0], g, in_sem.at[0]),
        pltpu.make_async_copy(rs_hbm.at[0], rs, in_sem.at[1]),
        pltpu.make_async_copy(ls_hbm.at[0], ls, in_sem.at[2]),
    ]
    for copy in loads:
        copy.start()
    barrier = pltpu.get_barrier_semaphore()
    greeted = [to_y(d) for d in YORD] + [to_z(e) for e in ZORD] + [to_x(d) for d in XORD]
    for device in greeted:
        pl.semaphore_signal(barrier, inc=1, device_id=device, device_id_type=MESH)

    sx, sl = {}, {}

    def right_over_x(q):
        for k in range(NCH):
            for d in XORD:
                at = pl.multiple_of(at_x(d) * XP + k * CR, 8)
                sx[q, k, d] = send(
                    rp.at[q, pl.ds(at, CR), :], xr.at[q, k, d - 1],
                    x_s.at[q, k, d - 1], x_r.at[q, k, d - 1], to_x(d),
                )

    loads[0].wait()
    tile = g[...]
    gh, gl = split(tile)
    th, tl = split(tile.T)
    gs[0], gs[1] = gh, gl

    def right_gram(q):
        cols = slice(q * BLK, (q + 1) * BLK)
        pack(rp.at[q], mm((th[cols], tl[cols]), (gh[:, cols], gl[:, cols])))

    right_gram(0)
    pl.semaphore_wait(barrier, len(greeted))
    right_over_x(0)
    pack(lp, mm((gh, gl), (th, tl)))
    for d in YORD:
        at = pl.multiple_of(at_y(d) * LP, 8)
        sl[d] = send(lp.at[pl.ds(at, LP), :], lrecv.at[d - 1], ly_s.at[d - 1], ly_r.at[d - 1], to_y(d))
    right_gram(1)
    right_over_x(1)

    sz = {}

    def right_over_z(q):
        for k in range(NCH):
            total = rp[q, pl.ds(pl.multiple_of(x * XP + k * CR, 8), CR), :]
            for d in XORD:
                sx[q, k, d].wait_recv()
                total = total + xr[q, k, d - 1]
            zs[q, k] = total
            for e in ZORD:
                sz[q, k, e] = send(
                    zs.at[q, k], zr.at[q, k, e - 1], z_s.at[q, k, e - 1], z_r.at[q, k, e - 1], to_z(e)
                )

    gx = {}

    def right_gather(q):
        for k in range(NCH):
            total = zs[q, k]
            for e in (1, 3, 2):
                sz[q, k, e].wait_recv()
                total = total + zr[q, k, e - 1]
            here = pl.ds(pl.multiple_of(x * XP + k * CR, 8), CR)
            rag[q, here, :] = total
            for d in XORD:
                gx[q, k, d] = send(
                    rag.at[q, here, :], rag.at[q, here, :], gx_s.at[q, k, d - 1], gx_r.at[q, k, d - 1], to_x(d)
                )

    right_over_z(0)
    right_over_z(1)

    at = pl.multiple_of(col * LP, 8)
    total = lp[pl.ds(at, LP), :]
    for d in YORD:
        sl[d].wait_recv()
        total = total + lrecv[d - 1]
    lag[pl.ds(at, LP), :] = total
    sg = {}
    for d in YORD:
        sg[d] = send(lag.at[pl.ds(at, LP), :], lag.at[pl.ds(at, LP), :], lg_s.at[d - 1], lg_r.at[d - 1], to_y(d))

    def left_arrived():
        for d in YORD:
            sg[d].wait_recv()

    def right_arrived(q):
        for k in range(NCH):
            for d in XORD:
                gx[q, k, d].wait_recv()

    def stats_of(q):
        return unpack(rag.at[q]), rs[q * BLK : (q + 1) * BLK, :]

    su = {}

    def emit(q, root):
        cols = slice(q * BLK, (q + 1) * BLK)
        upd[q] = mm(split(half(cols)), split(root))
        lanes = pl.ds(pl.multiple_of(col * 2 * BLK + q * BLK, BLK), BLK)
        for d in YORD:
            at = pl.multiple_of(at_y(d) * 32, 32)
            su[q, d] = send(
                upd.at[q, pl.ds(at, 32), :], o_ref.at[0, :, lanes], u_s.at[q, d - 1], u_r.at[q, d - 1], to_y(d)
            )
        mine = pltpu.make_async_copy(
            upd.at[q, pl.ds(pl.multiple_of(col * 32, 32), 32), :], o_ref.at[0, :, lanes], out_sem.at[q]
        )
        mine.start()
        su[q, 0] = mine

    loads[1].wait()
    loads[2].wait()
    right_gather(0)
    right_gather(1)
    left_arrived()
    right_arrived(0)
    left, right = newton((unpack(lag), ls[...]), stats_of(0))
    left = split(left)

    def half(cols):
        return mm(left, (gs[0, :, cols], gs[1, :, cols]))

    emit(0, right)
    right_arrived(1)
    (right,) = newton(stats_of(1))
    emit(1, right)

    for q in range(2):
        su[q, 0].wait()
        for d in YORD:
            su[q, d].wait_recv()
    for group in (sx, sl, sz, sg, gx):
        for copy in group.values():
            copy.wait_send()
    for (q, d), copy in su.items():
        if d:
            copy.wait_send()


def per_device(grads, left_stats, right_stats):
    dma = pltpu.SemaphoreType.DMA
    return pl.pallas_call(
        kernel,
        out_shape=pltpu.VMEM((1, 32, D), F32),
        in_specs=[pl.BlockSpec(memory_space=pl.ANY)] * 3,
        out_specs=pl.BlockSpec(memory_space=pltpu.VMEM),
        scratch_shapes=[
            pltpu.VMEM((BLK, 2 * BLK), F32),
            pltpu.VMEM((BLK, BLK), F32),
            pltpu.VMEM((2 * BLK, BLK), F32),
            pltpu.VMEM((2, BLK, 2 * BLK), BF16),
            pltpu.VMEM((PACK, H), F32),
            pltpu.VMEM((2, PACK, H), F32),
            pltpu.VMEM((NY - 1, LP, H), F32),
            pltpu.VMEM((2, NCH, NX - 1, CR, H), F32),
            pltpu.VMEM((2, NCH, CR, H), F32),
            pltpu.VMEM((2, NCH, NZ - 1, CR, H), F32),
            pltpu.VMEM((PACK, H), F32),
            pltpu.VMEM((2, PACK, H), F32),
            pltpu.VMEM((2, BLK, BLK), F32),
            dma((3,)), dma((2,)),
            dma((NY - 1,)), dma((NY - 1,)), dma((NY - 1,)), dma((NY - 1,)),
            dma((2, NCH, NX - 1)), dma((2, NCH, NX - 1)),
            dma((2, NCH, NZ - 1)), dma((2, NCH, NZ - 1)),
            dma((2, NCH, NX - 1)), dma((2, NCH, NX - 1)),
            dma((2, NY - 1)), dma((2, NY - 1)),
        ],
        compiler_params=pltpu.CompilerParams(collective_id=0, has_side_effects=True),
        name="shampoo",
    )(grads, left_stats, right_stats)


def solution(mesh):
    return jax.shard_map(
        per_device,
        mesh=mesh,
        in_specs=(P("mat", "row", "col"), P("mat", "row", None), P("mat", "col", None)),
        out_specs=P("mat", ("row", "col"), None),
        check_vma=False,
    )
```

time: 47.8 us -> 45.2 us (0.946)
  the two profiles are of different devices: /device:TPU:64 before, /device:TPU:8 now
where the time goes in v2:
time: 45.2 us; the launch traced here: 45 us
  Pallas kernels  44.2 us (98%)
  local copies, waits for them, and re-layouts  0.8 us (2%)
    pallas_call x1, Pallas kernels, per_device(): pl.pallas_call(kernel, out_shape=pltpu.VMEM((1, 32, D), F32), in_specs=[p...  44.2 us

profile of v2, /device:TPU:8, one launch (start us, length us, event | category | flops | bytes accessed | tf_op | source)
XLA Modules:
  0.0 45.0 jit_solution(16667766784929516811)
XLA Ops:
  0.0 44.2 %shampoo.1 = f32[1,32,4096]{2,1,0:T(8,128)S(1)} custom-call(f32[1,256,512]{2,1,0:T(8,128)} %g_hbm.1, f32[1,256,256]{2,1,0:T(8,128)} %ls_hbm.1, f32[1,512,256]{2,1,0:T(8,128)} %rs_hbm.1), custom_call_target="tpu_custom_call" | custom-call | tf_op jit(solution)/shard_map/shampoo/pallas_call | solution.py:253
  44.2 0.8 %copy.5 = f32[1,32,4096]{2,1,0:T(8,128)} copy(f32[1,32,4096]{2,1,0:T(8,128)S(1)} %shampoo.1) | data formatting | bytes 1048576

commit v3 on v2

--- a/solution.py
+++ b/solution.py
@@ -12,11 +12,10 @@
 BETA, EPS = 0.5, 0.001
 F32, BF16 = jnp.float32, jnp.bfloat16
 MESH = pl.DeviceIdType.MESH
-PACK = 3 * H
-XP = PACK // NX
-NCH = 2
-CR = XP // NCH
-LP = PACK // NY
+PACK = 2 * H + 8
+XS, YS = 2 * H // NX, 2 * H // NY
+CR, LP = XS + 8, YS + 8
+NCH = 1
 YORD = (4, 3, 5, 2, 6, 1, 7)
 XORD = (2, 1, 3)
 ZORD = (2, 1, 3)
@@ -36,21 +35,37 @@
 
 
 def pack(ref, v):
-    ref[0:H, :] = v[:H, :H]
-    ref[H : 2 * H, :] = v[:H, H:]
-    ref[2 * H : 3 * H, :] = v[H:, H:]
-
-
-def unpack(ref):
-    a, b, d = ref[0:H, :], ref[H : 2 * H, :], ref[2 * H : 3 * H, :]
+    rows, cols = index(H)
+    low = v[H:, H:]
+    ref[0:H, :] = v[:H, H:]
+    ref[H : 2 * H, :] = jnp.where(rows >= cols, v[:H, :H], low)
+    diagonal = jnp.sum(jnp.where(rows == cols, low, 0.0), axis=0, keepdims=True)
+    ref[2 * H : PACK, :] = jnp.broadcast_to(diagonal, (8, H))
+
+
+def unpack(pieces, step):
+    count = pieces.shape[0]
+    lines = jnp.concatenate([pieces[i, 0:step, :] for i in range(count)], axis=0)
+    diagonal = pieces[count - 1, step : step + 1, :]
+    rows, cols = index(H)
+    b, both = lines[:H], lines[H:]
+    turned = both.T
+    a = jnp.where(rows >= cols, both, turned)
+    d = jnp.where(rows < cols, both, jnp.where(rows > cols, turned, diagonal))
     top = jnp.concatenate([a, b], axis=1)
     low = jnp.concatenate([b.T, d], axis=1)
     return jnp.concatenate([top, low], axis=0)
 
 
+def index(size):
+    return (
+        lax.broadcasted_iota(jnp.int32, (size, size), 0),
+        lax.broadcasted_iota(jnp.int32, (size, size), 1),
+    )
+
+
 def eye():
-    rows = lax.broadcasted_iota(jnp.int32, (BLK, BLK), 0)
-    cols = lax.broadcasted_iota(jnp.int32, (BLK, BLK), 1)
+    rows, cols = index(BLK)
     return jnp.where(rows == cols, 1.0, 0.0).astype(F32)
 
 
@@ -74,10 +89,12 @@
 
 def kernel(
     g_hbm, ls_hbm, rs_hbm, o_ref,
-    g, ls, rs, gs, lp, rp, lrecv, xr, zs, zr, lag, rag, upd,
-    in_sem, out_sem, ly_s, ly_r, lg_s, lg_r, x_s, x_r, z_s, z_r, gx_s, gx_r, u_s, u_r,
+    g, ls, rs, gs, hs, rr, lp, rp, lrecv, xr, zs, zr, lag, rag, upd,
+    go_sem, in_sem, out_sem, ly_s, ly_r, lg_s, lg_r, x_s, x_r, z_s, z_r, gx_s, gx_r, u_s, u_r,
 ):
-    row, col = lax.axis_index("row"), lax.axis_index("col")
+    row, col, mat = lax.axis_index("row"), lax.axis_index("col"), lax.axis_index("mat")
+    core = lax.rem(mat, 2)
+    twin = {"row": row, "col": col, "mat": mat + 1 - 2 * core}
     x, zh = row // NZ, lax.rem(row, NZ)
 
     def at_x(d):
@@ -98,10 +115,13 @@
     def to_y(d):
         return {"row": row, "col": at_y(d)}
 
-    def send(src, dst, ss, rs_, device):
-        copy = pltpu.make_async_remote_copy(
+    def remote(src, dst, ss, rs_, device):
+        return pltpu.make_async_remote_copy(
             src_ref=src, dst_ref=dst, send_sem=ss, recv_sem=rs_, device_id=device, device_id_type=MESH
         )
+
+    def send(src, dst, ss, rs_, device):
+        copy = remote(src, dst, ss, rs_, device)
         copy.start()
         return copy
 
@@ -113,7 +133,7 @@
     for copy in loads:
         copy.start()
     barrier = pltpu.get_barrier_semaphore()
-    greeted = [to_y(d) for d in YORD] + [to_z(e) for e in ZORD] + [to_x(d) for d in XORD]
+    greeted = [to_y(d) for d in YORD] + [to_z(e) for e in ZORD] + [to_x(d) for d in XORD] + [twin]
     for device in greeted:
         pl.semaphore_signal(barrier, inc=1, device_id=device, device_id_type=MESH)
 
@@ -122,8 +142,8 @@
     def right_over_x(q):
         for k in range(NCH):
             for d in XORD:
-                at = pl.multiple_of(at_x(d) * XP + k * CR, 8)
-                sx[q, k, d] = send(
+                at = pl.multiple_of(at_x(d) * XS, 8)
+                sx[q, k, d] = remote(
                     rp.at[q, pl.ds(at, CR), :], xr.at[q, k, d - 1],
                     x_s.at[q, k, d - 1], x_r.at[q, k, d - 1], to_x(d),
                 )
@@ -138,21 +158,29 @@
         cols = slice(q * BLK, (q + 1) * BLK)
         pack(rp.at[q], mm((th[cols], tl[cols]), (gh[:, cols], gl[:, cols])))
 
+    def start_x(q):
+        for d in XORD:
+            sx[q, 0, d].start()
+
+    right_over_x(0)
+    right_over_x(1)
     right_gram(0)
     pl.semaphore_wait(barrier, len(greeted))
-    right_over_x(0)
+    pl.when(core == 1)(lambda: start_x(0))
     pack(lp, mm((gh, gl), (th, tl)))
     for d in YORD:
-        at = pl.multiple_of(at_y(d) * LP, 8)
+        at = pl.multiple_of(at_y(d) * YS, 8)
         sl[d] = send(lp.at[pl.ds(at, LP), :], lrecv.at[d - 1], ly_s.at[d - 1], ly_r.at[d - 1], to_y(d))
     right_gram(1)
-    right_over_x(1)
+    pl.when(core == 0)(lambda: pl.semaphore_wait(go_sem, 1))
+    pl.when(core == 0)(lambda: start_x(0))
+    start_x(1)
 
     sz = {}
 
     def right_over_z(q):
         for k in range(NCH):
-            total = rp[q, pl.ds(pl.multiple_of(x * XP + k * CR, 8), CR), :]
+            total = rp[q, pl.ds(pl.multiple_of(x * XS, 8), CR), :]
             for d in XORD:
                 sx[q, k, d].wait_recv()
                 total = total + xr[q, k, d - 1]
@@ -170,25 +198,29 @@
             for e in (1, 3, 2):
                 sz[q, k, e].wait_recv()
                 total = total + zr[q, k, e - 1]
-            here = pl.ds(pl.multiple_of(x * XP + k * CR, 8), CR)
-            rag[q, here, :] = total
+            rag[q, x] = total
             for d in XORD:
                 gx[q, k, d] = send(
-                    rag.at[q, here, :], rag.at[q, here, :], gx_s.at[q, k, d - 1], gx_r.at[q, k, d - 1], to_x(d)
+                    rag.at[q, x], rag.at[q, x], gx_s.at[q, k, d - 1], gx_r.at[q, k, d - 1], to_x(d)
                 )
 
     right_over_z(0)
+
+    @pl.when(core == 1)
+    def _():
+        pl.semaphore_signal(go_sem, inc=1, device_id=twin, device_id_type=MESH)
+
     right_over_z(1)
 
-    at = pl.multiple_of(col * LP, 8)
+    at = pl.multiple_of(col * YS, 8)
     total = lp[pl.ds(at, LP), :]
     for d in YORD:
         sl[d].wait_recv()
         total = total + lrecv[d - 1]
-    lag[pl.ds(at, LP), :] = total
+    lag[col] = total
     sg = {}
     for d in YORD:
-        sg[d] = send(lag.at[pl.ds(at, LP), :], lag.at[pl.ds(at, LP), :], lg_s.at[d - 1], lg_r.at[d - 1], to_y(d))
+        sg[d] = send(lag.at[col], lag.at[col], lg_s.at[d - 1], lg_r.at[d - 1], to_y(d))
 
     def left_arrived():
         for d in YORD:
@@ -200,13 +232,13 @@
                 gx[q, k, d].wait_recv()
 
     def stats_of(q):
-        return unpack(rag.at[q]), rs[q * BLK : (q + 1) * BLK, :]
+        return unpack(rag.at[q], XS), rs[q * BLK : (q + 1) * BLK, :]
 
     su = {}
 
     def emit(q, root):
         cols = slice(q * BLK, (q + 1) * BLK)
-        upd[q] = mm(split(half(cols)), split(root))
+        upd[q] = mm(split(hs[:, cols]), split(root))
         lanes = pl.ds(pl.multiple_of(col * 2 * BLK + q * BLK, BLK), BLK)
         for d in YORD:
             at = pl.multiple_of(at_y(d) * 32, 32)
@@ -222,16 +254,27 @@
     loads[1].wait()
     loads[2].wait()
     right_gather(0)
+
+    @pl.when(core == 0)
+    def _():
+        left_arrived()
+        (left,) = newton((unpack(lag, YS), ls[...]))
+        hs[...] = mm(split(left), (gs[0], gs[1]))
+
     right_gather(1)
-    left_arrived()
     right_arrived(0)
-    left, right = newton((unpack(lag), ls[...]), stats_of(0))
-    left = split(left)
-
-    def half(cols):
-        return mm(left, (gs[0, :, cols], gs[1, :, cols]))
-
-    emit(0, right)
+
+    @pl.when(core == 0)
+    def _():
+        (rr[...],) = newton(stats_of(0))
+
+    @pl.when(core == 1)
+    def _():
+        left_arrived()
+        left, rr[...] = newton((unpack(lag, YS), ls[...]), stats_of(0))
+        hs[...] = mm(split(left), (gs[0], gs[1]))
+
+    emit(0, rr[...])
     right_arrived(1)
     (right,) = newton(stats_of(1))
     emit(1, right)
@@ -260,15 +303,18 @@
             pltpu.VMEM((BLK, BLK), F32),
             pltpu.VMEM((2 * BLK, BLK), F32),
             pltpu.VMEM((2, BLK, 2 * BLK), BF16),
+            pltpu.VMEM((BLK, 2 * BLK), F32),
+            pltpu.VMEM((BLK, BLK), F32),
             pltpu.VMEM((PACK, H), F32),
             pltpu.VMEM((2, PACK, H), F32),
             pltpu.VMEM((NY - 1, LP, H), F32),
             pltpu.VMEM((2, NCH, NX - 1, CR, H), F32),
             pltpu.VMEM((2, NCH, CR, H), F32),
             pltpu.VMEM((2, NCH, NZ - 1, CR, H), F32),
-            pltpu.VMEM((PACK, H), F32),
-            pltpu.VMEM((2, PACK, H), F32),
+            pltpu.VMEM((NY, LP, H), F32),
+            pltpu.VMEM((2, NX, CR, H), F32),
             pltpu.VMEM((2, BLK, BLK), F32),
+            pltpu.SemaphoreType.REGULAR,
             dma((3,)), dma((2,)),
             dma((NY - 1,)), dma((NY - 1,)), dma((NY - 1,)), dma((NY - 1,)),
             dma((2, NCH, NX - 1)), dma((2, NCH, NX - 1)),

time: 45.2 us -> 42.9 us (0.949)
  Pallas kernels: 44.2 us -> 41.9 us
    pallas_call x1, Pallas kernels: 44.2 us -> 41.9 us  [per_device(): pl.pallas_call(kernel, out_shape=pltpu.VMEM((1, 32, D), F32), in_specs=[p...]
where the time goes in v3:
time: 42.9 us; the launch traced here: 42.8 us
  Pallas kernels  41.9 us (98%)
  local copies, waits for them, and re-layouts  0.8 us (2%)
    pallas_call x1, Pallas kernels, per_device(): pl.pallas_call(kernel, out_shape=pltpu.VMEM((1, 32, D), F32), in_specs=[p...  41.9 us

profile of v3, /device:TPU:8, one launch (start us, length us, event | category | flops | bytes accessed | tf_op | source)
XLA Modules:
  0.0 42.8 jit_solution(11597978142520922746)
XLA Ops:
  0.0 41.9 %shampoo.1 = f32[1,32,4096]{2,1,0:T(8,128)S(1)} custom-call(f32[1,256,512]{2,1,0:T(8,128)} %g_hbm.1, f32[1,256,256]{2,1,0:T(8,128)} %ls_hbm.1, f32[1,512,256]{2,1,0:T(8,128)} %rs_hbm.1), custom_call_target="tpu_custom_call" | custom-call | tf_op jit(solution)/shard_map/shampoo/pallas_call | solution.py:296
  42.0 0.8 %copy.5 = f32[1,32,4096]{2,1,0:T(8,128)} copy(f32[1,32,4096]{2,1,0:T(8,128)S(1)} %shampoo.1) | data formatting | bytes 1048576

commit v4 on v3

--- a/solution.py
+++ b/solution.py
@@ -126,7 +126,8 @@
         return copy
 
     loads = [
-        pltpu.make_async_copy(g_hbm.at[0], g, in_sem.at[0]),
+        pltpu.make_async_copy(g_hbm.at[0, :, 0:BLK], g.at[:, 0:BLK], in_sem.at[0]),
+        pltpu.make_async_copy(g_hbm.at[0, :, BLK : 2 * BLK], g.at[:, BLK : 2 * BLK], in_sem.at[3]),
         pltpu.make_async_copy(rs_hbm.at[0], rs, in_sem.at[1]),
         pltpu.make_async_copy(ls_hbm.at[0], ls, in_sem.at[2]),
     ]
@@ -148,15 +149,17 @@
                     x_s.at[q, k, d - 1], x_r.at[q, k, d - 1], to_x(d),
                 )
 
-    loads[0].wait()
-    tile = g[...]
-    gh, gl = split(tile)
-    th, tl = split(tile.T)
-    gs[0], gs[1] = gh, gl
+    parts = {}
+
+    def take(q):
+        cols = slice(q * BLK, (q + 1) * BLK)
+        tile = g[:, cols]
+        parts[q] = split(tile), split(tile.T)
+        gs[0, :, cols], gs[1, :, cols] = parts[q][0]
 
     def right_gram(q):
-        cols = slice(q * BLK, (q + 1) * BLK)
-        pack(rp.at[q], mm((th[cols], tl[cols]), (gh[:, cols], gl[:, cols])))
+        held, turned = parts[q]
+        pack(rp.at[q], mm(turned, held))
 
     def start_x(q):
         for d in XORD:
@@ -164,10 +167,14 @@
 
     right_over_x(0)
     right_over_x(1)
+    loads[0].wait()
+    take(0)
     right_gram(0)
     pl.semaphore_wait(barrier, len(greeted))
     pl.when(core == 1)(lambda: start_x(0))
-    pack(lp, mm((gh, gl), (th, tl)))
+    loads[1].wait()
+    take(1)
+    pack(lp, mm(*parts[0]) + mm(*parts[1]))
     for d in YORD:
         at = pl.multiple_of(at_y(d) * YS, 8)
         sl[d] = send(lp.at[pl.ds(at, LP), :], lrecv.at[d - 1], ly_s.at[d - 1], ly_r.at[d - 1], to_y(d))
@@ -251,8 +258,8 @@
         mine.start()
         su[q, 0] = mine
 
-    loads[1].wait()
     loads[2].wait()
+    loads[3].wait()
     right_gather(0)
 
     @pl.when(core == 0)
@@ -315,7 +322,7 @@
             pltpu.VMEM((2, NX, CR, H), F32),
             pltpu.VMEM((2, BLK, BLK), F32),
             pltpu.SemaphoreType.REGULAR,
-            dma((3,)), dma((2,)),
+            dma((4,)), dma((2,)),
             dma((NY - 1,)), dma((NY - 1,)), dma((NY - 1,)), dma((NY - 1,)),
             dma((2, NCH, NX - 1)), dma((2, NCH, NX - 1)),
             dma((2, NCH, NZ - 1)), dma((2, NCH, NZ - 1)),

time: 42.9 us -> 42.6 us (level)
  no operation moved by 1% of the time
where the time goes in v4:
time: 42.6 us; the launch traced here: 42.4 us
  Pallas kernels  41.6 us (98%)
  local copies, waits for them, and re-layouts  0.8 us (2%)
    pallas_call x1, Pallas kernels, per_device(): pl.pallas_call(kernel, out_shape=pltpu.VMEM((1, 32, D), F32), in_specs=[p...  41.6 us

profile of v4, /device:TPU:8, one launch (start us, length us, event | category | flops | bytes accessed | tf_op | source)
XLA Modules:
  0.0 42.4 jit_solution(17313229204113854755)
XLA Ops:
  0.0 41.6 %shampoo.1 = f32[1,32,4096]{2,1,0:T(8,128)S(1)} custom-call(f32[1,256,512]{2,1,0:T(8,128)} %g_hbm.1, f32[1,256,256]{2,1,0:T(8,128)} %ls_hbm.1, f32[1,512,256]{2,1,0:T(8,128)} %rs_hbm.1), custom_call_target="tpu_custom_call" | custom-call | tf_op jit(solution)/shard_map/shampoo/pallas_call | solution.py:303
  41.6 0.8 %copy.5 = f32[1,32,4096]{2,1,0:T(8,128)} copy(f32[1,32,4096]{2,1,0:T(8,128)S(1)} %shampoo.1) | data formatting | bytes 1048576
